TPU v7x, 32 devices: a whole 2x2x4 slice. The times are simulated.
32 devices in a mesh: dp: 2 (over x), row: 4 (over z), col: 4 (over y, core).
Axes of the slice: x: 2, y: 2, z: 4, core: 2. Of those that a mesh axis runs over, the one named last changes fastest.
Arguments:
- stash_codes: int32 [1024, 4096], P(('dp', 'col'), 'row'), may hold values from 0 to 3
- stash_scales: int32 [1024, 32], P(('dp', 'col'), 'row'), may hold values from 1 to 8
- pad_mask: int32 [1024], P(('dp', 'col')), may hold values 0 or 1
- cotangent: bfloat16 [1024, 4096], P(('dp', 'col'), 'row'), may hold values from -3 to 3
- w_gate: bfloat16 [4096, 10240], P('row', 'col'), may hold values from -0.09375 to 0.09375
- w_up: bfloat16 [4096, 10240], P('row', 'col'), may hold values from -0.09375 to 0.09375
- w_out: bfloat16 [4096, 10240], P('row', 'col'), may hold values from -0.09375 to 0.09375
Outputs:
- input_grad: float32 [1024, 4096], P(('dp', 'col'), 'row')
- gate_weight_grad: float32 [4096, 10240], P('row', 'col')
- up_weight_grad: float32 [4096, 10240], P('row', 'col')
- out_weight_grad: float32 [4096, 10240], P('row', 'col')
All inputs are finite; a program needn't handle non-finite values. No bound on the sum of `pad_mask` on one device may be relied on, other than what follows from the above.
Results may differ from a plain program's by a relative error of at most 0.0029.
Values may be sent and summed in bfloat16 or wider, within the bound.
No kernel may reach another device: no remote copies, remote signals or barrier semaphores. Data moves between devices by JAX's collectives and lax.ppermute only.
A program may use at most 192 MiB of HBM per device.

v0:
```python
import jax
import jax.numpy as jnp
from jax import lax
from jax.sharding import PartitionSpec as P

root_term = 0.7978845608028654
cubic_term = 0.044715


def gelu_pair(values):
    inside = root_term * (values + cubic_term * values * values * values)
    tangent = jnp.tanh(inside)
    activated = 0.5 * values * (1.0 + tangent)
    derivative = 0.5 * (1.0 + tangent) + 0.5 * values * (1.0 - tangent * tangent) * root_term * (
        1.0 + 3.0 * cubic_term * values * values
    )
    return (activated, derivative)


def unpack_stash(stash_codes, stash_scales):
    blocks = stash_scales.shape[1]
    block_width = stash_codes.shape[1] // blocks
    levels = (
        (2 * stash_codes - 3).astype(jnp.float32).reshape(stash_codes.shape[0], blocks, block_width)
    )
    scaled = levels * stash_scales.astype(jnp.float32)[:, :, None] / 16.0
    return scaled.reshape(stash_codes.shape).astype(jnp.bfloat16)


def per_device(stash_codes, stash_scales, pad_mask, cotangent, w_gate, w_up, w_out):
    stashed = unpack_stash(stash_codes, stash_scales)
    live_grad = (cotangent.astype(jnp.float32) * pad_mask.astype(jnp.float32)[:, None]).astype(
        jnp.bfloat16
    )
    stash_all, grad_all = (
        lax.all_gather(stashed, "col", axis=0, tiled=True),
        lax.all_gather(live_grad, "col", axis=0, tiled=True),
    )
    ff_local = w_gate.shape[1]
    joined = lax.psum_scatter(
        jnp.concatenate(
            [
                jnp.dot(stash_all, w_gate, preferred_element_type=jnp.float32),
                jnp.dot(stash_all, w_up, preferred_element_type=jnp.float32),
                jnp.dot(grad_all, w_out, preferred_element_type=jnp.float32),
            ],
            axis=1,
        ),
        "row",
        scatter_dimension=0,
        tiled=True,
    )
    gate_pre = joined[:, :ff_local]
    up_part = joined[:, ff_local : 2 * ff_local]
    back_grad = joined[:, 2 * ff_local :]
    activated, derivative = gelu_pair(gate_pre)
    hidden = (activated * up_part).astype(jnp.bfloat16)
    gate_grad = (back_grad * up_part * derivative).astype(jnp.bfloat16)
    up_grad = (back_grad * activated).astype(jnp.bfloat16)
    local_stack = jnp.concatenate([gate_grad, up_grad, hidden], axis=1)
    stacked = lax.all_gather(local_stack, "row", axis=0, tiled=True)
    transposed = (((1,), (1,)), ((), ()))
    gate_rows = stacked[:, :ff_local]
    up_rows = stacked[:, ff_local : 2 * ff_local]
    input_grad = lax.psum_scatter(
        lax.dot_general(gate_rows, w_gate, transposed, preferred_element_type=jnp.float32)
        + lax.dot_general(up_rows, w_up, transposed, preferred_element_type=jnp.float32),
        "col",
        scatter_dimension=0,
        tiled=True,
    )
    contract = (((0,), (0,)), ((), ()))
    inputs_part = lax.dot_general(
        stash_all, stacked[:, : 2 * ff_local], contract, preferred_element_type=jnp.float32
    )
    second = lax.dot_general(
        grad_all, stacked[:, 2 * ff_local :], contract, preferred_element_type=jnp.float32
    )
    summed = lax.psum(jnp.concatenate([inputs_part, second], axis=1), "dp")
    return (
        input_grad,
        summed[:, :ff_local],
        summed[:, ff_local : 2 * ff_local],
        summed[:, 2 * ff_local :],
    )


def solution(mesh):
    return jax.shard_map(
        per_device,
        mesh=mesh,
        in_specs=(
            P(("dp", "col"), "row"),
            P(("dp", "col"), "row"),
            P(("dp", "col")),
            P(("dp", "col"), "row"),
            P("row", "col"),
            P("row", "col"),
            P("row", "col"),
        ),
        out_specs=(P(("dp", "col"), "row"), P("row", "col"), P("row", "col"), P("row", "col")),
        check_vma=False,
    )
```

profile of v0, /device:TPU:0, one launch (start us, length us, event | category | flops | bytes accessed | tf_op | source)
XLA Modules:
  0.0 1232.1 jit_solution(16199917067725401654)
XLA Ops:
  7.2 0.0 all-gather.4.cloned.1.call-start
  7.2 0.7 convert_element_type.28
  7.9 0.1 copy.11
  8.0 0.2 mul.85
  8.2 1.9 fusion.19
  10.1 0.0 all-gather.4.cloned.1.call-update
  10.1 0.0 all-gather.6.cloned.1.call-start
  10.2 0.7 convert_element_type.31
  10.9 1.8 multiply_convert_fusion.2
  12.6 0.0 all-gather.6.cloned.1.call-update
  12.6 0.0 reduce-scatter.3.cloned.1.call-start
  12.7 17.0 %all-gather.4.cloned.1.call-done = bf16[512,1024]{1,0:T(8,128)(2,1)} async-done(((bf16[128,1024]{1,0:T(8,128)(2,1)}), bf16[512,1024]{1,0:T(8,128)(2,1)}) %all-gather.4.cloned.1.call-update) | async-done | bytes 1048592 | tf_op jit(solution)/shard_map/all_gather | solution.py:36
  29.7 0.0 copy-start.2
  29.7 8.1 fusion.22
  37.9 0.0 copy-done.2
  37.9 7.3 fusion.21
  45.1 3.5 all-gather.6.cloned.1.call-done
  48.6 0.0 copy-start
  48.6 0.0 copy-start.1
  48.6 5.2 fusion.23
  53.8 0.0 copy-done
  53.9 0.7 copy-done.1
  54.5 5.8 pad_maximum_fusion.1
  60.3 0.0 reduce-scatter.3.cloned.1.call-update
  60.3 0.0 copy-start.3
  60.3 0.0 all-gather.8.cloned.1.call-start
  60.4 262.7 %reduce-scatter.3.cloned.1.call-done = f32[128,7680]{1,0:T(8,128)} async-done(((f32[512,7680]{1,0:T(8,128)}), f32[128,7680]{1,0:T(8,128)}) %reduce-scatter.3.cloned.1.call-update) | async-done | bytes 3932176 | tf_op jit(solution)/shard_map/reduce_scatter | solution.py:40
  323.1 3.2 fusion.17
  326.3 1.4 pad_maximum_fusion.2
  327.7 0.0 all-gather.8.cloned.1.call-update
  327.7 0.0 all-reduce.2.cloned.1.call-start
  327.8 142.2 %all-gather.8.cloned.1.call-done = bf16[512,7680]{1,0:T(8,128)(2,1)} async-done(((bf16[128,7680]{1,0:T(8,128)(2,1)}), bf16[512,7680]{1,0:T(8,128)(2,1)}) %all-gather.8.cloned.1.call-update) | async-done | bytes 7864336 | tf_op jit(solution)/shard_map/all_gather | solution.py:61
  469.9 0.0 copy-done.3
  469.9 7.4 fusion.2
  477.3 7.6 fusion
  485.0 14.9 %pad_maximum_fusion = f32[1024,7680]{1,0:T(8,128)} fusion(f32[1024,2560]{1,0:T(8,128)} %fusion.2, f32[1024,5120]{1,0:T(8,128)S(1)} %fusion), kind=kLoop, calls=%fused_computation | loop fusion | flops 7864320 | bytes 62914560 | tf_op jit(solution)/shard_map/concatenate | solution.py:79
  499.9 0.0 all-reduce.2.cloned.1.call-update
  499.9 0.2 reduce-scatter.5.cloned.1.call-start
  500.1 5.7 fusion.4
  505.8 7.5 fusion.8
  513.3 0.0 reduce-scatter.5.cloned.1.call-update
  513.4 677.7 %all-reduce.2.cloned.1.call-done = f32[1024,7680]{1,0:T(8,128)} async-done(((f32[1024,7680]{1,0:T(8,128)}), f32[1024,7680]{1,0:T(8,128)}) %all-reduce.2.cloned.1.call-update) | async-done | bytes 31457296 | tf_op jit(solution)/shard_map/psum | solution.py:79
  1191.0 22.7 %fusion.20 = (f32[1024,2560]{1,0:T(8,128)}, f32[1024,2560]{1,0:T(8,128)}, f32[1024,2560]{1,0:T(8,128)}) fusion(f32[1024,7680]{1,0:T(8,128)} %all-reduce.2.cloned.1.call-done), kind=kLoop, calls=%fused_computation.28 | loop fusion | bytes 62914560 | tf_op jit(solution)/shard_map/slice | solution.py:84
  1213.7 11.5 reduce-scatter.5.cloned.1.call-done
Async XLA Ops:
  7.2 22.6 %all-gather.4.cloned.1.call-start = ((), (), s32[]{:S(2)}) async-start(), calls=%async_computation.2 | async-start | bytes 1310720 | tf_op jit(solution)/shard_map/all_gather | solution.py:36
  10.1 38.4 %all-gather.6.cloned.1.call-start = ((), (), s32[]{:S(2)}) async-start(), calls=%async_computation.3 | async-start | bytes 1310720 | tf_op jit(solution)/shard_map/all_gather | solution.py:37
  12.6 310.5 %reduce-scatter.3.cloned.1.call-start = ((), (), s32[]{:S(2)}) async-start(), calls=%async_computation.4 | async-start | bytes 19660800 | tf_op jit(solution)/shard_map/reduce_scatter | solution.py:40
  29.7 8.1 copy-start.2
  48.6 5.3 copy-start
  48.6 5.9 copy-start.1
  60.3 409.6 %copy-start.3 = (bf16[512,1024]{1,0:T(8,128)(2,1)S(1)}, bf16[512,1024]{1,0:T(8,128)(2,1)}, u32[]{:S(2)}) copy-start(bf16[512,1024]{1,0:T(8,128)(2,1)} %all-gather.6.cloned.1.call-done) | copy-start | bytes 3145732
  60.3 409.6 %all-gather.8.cloned.1.call-start = ((), (), s32[]{:S(2)}) async-start(), calls=%async_computation.5 | async-start | bytes 9830400 | tf_op jit(solution)/shard_map/all_gather | solution.py:61
  327.7 863.3 %all-reduce.2.cloned.1.call-start = ((), (), s32[]{:S(2)}) async-start(), calls=%async_computation.7 | async-start | bytes 62914560 | tf_op jit(solution)/shard_map/psum | solution.py:79
  499.9 725.3 %reduce-scatter.5.cloned.1.call-start = ((), (), s32[]{:S(2)}) async-start(), calls=%async_computation.6 | async-start | bytes 2621440 | tf_op jit(solution)/shard_map/reduce_scatter | solution.py:65
Sparse Core Ops, SparseCore 0:
  10.3 19.4 all-gather.3
  31.9 16.6 all-gather.5
  60.4 262.6 reduce-scatter.2
  327.8 142.0 all-gather.7
  500.0 690.9 all-reduce.1
  1194.0 31.1 reduce-scatter.4
where the time goes:
time: 1230 us
  waiting for transfers between devices  1110 us (90%)
  matrix products  48.9 us (4%)
  other arithmetic  30.3 us (2%)
  local copies, waits for them, and re-layouts  23.6 us (2%)
  between operations  14.2 us (1%)
    psum x1, waiting for transfers between devices, per_device(): summed = lax.psum(jnp.concatenate([inputs_part, second], axis=1), 'dp')  678 us
    reduce_scatter x1, waiting for transfers between devices, per_device(): lax.psum_scatter(jnp.concatenate([jnp.dot(stash_all, w_gate, preferred_el...  263 us
    all_gather x1, waiting for transfers between devices, per_device(): stacked = lax.all_gather(local_stack, 'row', axis=0, tiled=True)  142 us
  transfers between devices with their start and end apart: 6, of which 6 were waited for; matrix products, arithmetic and copies ran while one was open for 4% of the time, Pallas kernels for 0%

commit v1 on v0

--- a/solution.py
+++ b/solution.py
@@ -76,7 +76,7 @@
     second = lax.dot_general(
         grad_all, stacked[:, 2 * ff_local :], contract, preferred_element_type=jnp.float32
     )
-    summed = lax.psum(jnp.concatenate([inputs_part, second], axis=1), "dp")
+    summed = jnp.sum(lax.all_gather(jnp.concatenate([inputs_part, second], axis=1), "dp"), axis=0)
     return (
         input_grad,
         summed[:, :ff_local],

time: 1230 us -> 1280 us (1.041)
  other arithmetic: 30.3 us -> 64.3 us
  waiting for transfers between devices: 1110 us -> 1130 us
    all_gather x0 -> x1, waiting for transfers between devices: none -> 703 us  [per_device(): lax.all_gather(jnp.concatenate([inputs_part, second], axis=1), 'dp')]
    psum x1 -> x0, waiting for transfers between devices: 678 us -> none  [per_device(): summed = lax.psum(jnp.concatenate([inputs_part, second], axis=1), 'dp')]
    reduce_sum x0 -> x1, other arithmetic: none -> 34 us  [per_device(): jnp.sum(lax.all_gather(jnp.concatenate([inputs_part, second], axis=1), 'd...]
  transfers between devices with their start and end apart: 6 -> 6, of which waited for: 6 -> 5; matrix products, arithmetic and copies ran while one was open for 4% -> 7% of each run, Pallas kernels for 0% -> 0%
where the time goes in v1:
time: 1280 us
  waiting for transfers between devices  1130 us (88%)
  other arithmetic  64.3 us (5%)
  matrix products  51.8 us (4%)
  local copies, waits for them, and re-layouts  23.3 us (2%)
  between operations  14.2 us (1%)
    all_gather x1, waiting for transfers between devices, per_device(): lax.all_gather(jnp.concatenate([inputs_part, second], axis=1), 'dp')  703 us
    reduce_scatter x1, waiting for transfers between devices, per_device(): lax.psum_scatter(jnp.concatenate([jnp.dot(stash_all, w_gate, preferred_el...  263 us
    all_gather x1, waiting for transfers between devices, per_device(): stacked = lax.all_gather(local_stack, 'row', axis=0, tiled=True)  142 us
    reduce_sum x1, other arithmetic, per_device(): jnp.sum(lax.all_gather(jnp.concatenate([inputs_part, second], axis=1), 'd...  34 us
  transfers between devices with their start and end apart: 6, of which 5 were waited for; matrix products, arithmetic and copies ran while one was open for 7% of the time, Pallas kernels for 0%

profile of v1, /device:TPU:0, one launch (start us, length us, event | category | flops | bytes accessed | tf_op | source)
XLA Modules:
  0.0 1283.0 jit_solution(14442084789382581275)
XLA Ops:
  7.2 0.0 all-gather.6.cloned.1.call-start
  7.2 0.7 convert_element_type.28
  7.9 0.1 copy.11
  8.0 0.2 mul.85
  8.2 1.9 fusion.19
  10.1 0.0 all-gather.6.cloned.1.call-update
  10.1 0.0 all-gather.8.cloned.1.call-start
  10.2 0.7 convert_element_type.31
  10.9 1.8 multiply_convert_fusion.2
  12.6 0.0 all-gather.8.cloned.1.call-update
  12.6 0.0 reduce-scatter.3.cloned.1.call-start
  12.7 17.0 %all-gather.6.cloned.1.call-done = bf16[512,1024]{1,0:T(8,128)(2,1)} async-done(((bf16[128,1024]{1,0:T(8,128)(2,1)}), bf16[512,1024]{1,0:T(8,128)(2,1)}) %all-gather.6.cloned.1.call-update) | async-done | bytes 1048592 | tf_op jit(solution)/shard_map/all_gather | solution.py:36
  29.7 0.0 copy-start.2
  29.7 8.1 fusion.22
  37.9 0.0 copy-done.2
  37.9 7.3 fusion.21
  45.1 3.5 all-gather.8.cloned.1.call-done
  48.6 0.0 copy-start
  48.6 0.0 copy-start.1
  48.6 5.2 fusion.23
  53.8 0.0 copy-done
  53.9 0.7 copy-done.1
  54.5 5.8 pad_maximum_fusion.1
  60.3 0.0 reduce-scatter.3.cloned.1.call-update
  60.3 0.0 copy-start.3
  60.3 0.0 all-gather.10.cloned.1.call-start
  60.4 262.7 %reduce-scatter.3.cloned.1.call-done = f32[128,7680]{1,0:T(8,128)} async-done(((f32[512,7680]{1,0:T(8,128)}), f32[128,7680]{1,0:T(8,128)}) %reduce-scatter.3.cloned.1.call-update) | async-done | bytes 3932176 | tf_op jit(solution)/shard_map/reduce_scatter | solution.py:40
  323.1 3.2 fusion.17
  326.3 1.4 pad_maximum_fusion.2
  327.7 0.0 all-gather.10.cloned.1.call-update
  327.7 0.0 all-gather.12.cloned.1.call-start
  327.8 142.2 %all-gather.10.cloned.1.call-done = bf16[512,7680]{1,0:T(8,128)(2,1)} async-done(((bf16[128,7680]{1,0:T(8,128)(2,1)}), bf16[512,7680]{1,0:T(8,128)(2,1)}) %all-gather.10.cloned.1.call-update) | async-done | bytes 7864336 | tf_op jit(solution)/shard_map/all_gather | solution.py:61
  469.9 0.0 copy-done.3
  469.9 7.4 fusion.2
  477.3 7.6 fusion
  485.0 15.0 %pad_maximum_fusion = f32[1024,7680]{1,0:T(8,128)} fusion(f32[1024,2560]{1,0:T(8,128)} %fusion.2, f32[1024,5120]{1,0:T(8,128)S(1)} %fusion), kind=kLoop, calls=%fused_computation | loop fusion | flops 7864320 | bytes 62914560 | tf_op jit(solution)/shard_map/concatenate | solution.py:79
  499.9 0.0 all-gather.12.cloned.1.call-update
  499.9 0.2 reduce-scatter.5.cloned.1.call-start
  500.2 5.7 fusion.4
  505.9 10.5 fusion.8
  516.4 0.0 reduce-scatter.5.cloned.1.call-update
  516.4 703.5 %all-gather.12.cloned.1.call-done = f32[2048,7680]{1,0:T(8,128)} async-done(((f32[1024,7680]{1,0:T(8,128)}), f32[2048,7680]{1,0:T(8,128)}) %all-gather.12.cloned.1.call-update) | async-done | bytes 62914576 | tf_op jit(solution)/shard_map/all_gather | solution.py:79
  1219.9 34.0 %reduce_sum.9 = f32[1024,7680]{1,0:T(8,128)} reduce(f32[2,1024,7680]{2,1,0:T(8,128)} %bitcast.18, f32[]{:T(128)} %constant.19.clone.1), dimensions={0}, to_apply=%region_2.0 | reduce | flops 7864320 | bytes 94371840 | tf_op jit(solution)/shard_map/reduce_sum | solution.py:79
  1253.8 22.3 %fusion.20 = (f32[1024,2560]{1,0:T(8,128)}, f32[1024,2560]{1,0:T(8,128)}, f32[1024,2560]{1,0:T(8,128)}) fusion(f32[1024,7680]{1,0:T(8,128)} %reduce_sum.9), kind=kLoop, calls=%fused_computation.28 | loop fusion | bytes 62914560 | tf_op jit(solution)/shard_map/slice | solution.py:84
  1276.1 0.0 reduce-scatter.5.cloned.1.call-done
Async XLA Ops:
  7.2 22.6 %all-gather.6.cloned.1.call-start = ((), (), s32[]{:S(2)}) async-start(), calls=%async_computation.2 | async-start | bytes 1310720 | tf_op jit(solution)/shard_map/all_gather | solution.py:36
  10.1 38.4 %all-gather.8.cloned.1.call-start = ((), (), s32[]{:S(2)}) async-start(), calls=%async_computation.3 | async-start | bytes 1310720 | tf_op jit(solution)/shard_map/all_gather | solution.py:37
  12.6 310.5 %reduce-scatter.3.cloned.1.call-start = ((), (), s32[]{:S(2)}) async-start(), calls=%async_computation.4 | async-start | bytes 19660800 | tf_op jit(solution)/shard_map/reduce_scatter | solution.py:40
  29.7 8.1 copy-start.2
  48.6 5.3 copy-start
  48.6 5.9 copy-start.1
  60.3 409.6 %copy-start.3 = (bf16[512,1024]{1,0:T(8,128)(2,1)S(1)}, bf16[512,1024]{1,0:T(8,128)(2,1)}, u32[]{:S(2)}) copy-start(bf16[512,1024]{1,0:T(8,128)(2,1)} %all-gather.8.cloned.1.call-done) | copy-start | bytes 3145732
  60.3 409.6 %all-gather.10.cloned.1.call-start = ((), (), s32[]{:S(2)}) async-start(), calls=%async_computation.5 | async-start | bytes 9830400 | tf_op jit(solution)/shard_map/all_gather | solution.py:61
  327.7 892.1 %all-gather.12.cloned.1.call-start = ((), (), s32[]{:S(2)}) async-start(), calls=%async_computation.7 | async-start | bytes 94371840 | tf_op jit(solution)/shard_map/all_gather | solution.py:79
  499.9 776.2 %reduce-scatter.5.cloned.1.call-start = ((), (), s32[]{:S(2)}) async-start(), calls=%async_computation.6 | async-start | bytes 2621440 | tf_op jit(solution)/shard_map/reduce_scatter | solution.py:65
Sparse Core Ops, SparseCore 0:
  10.3 19.4 all-gather.5
  31.9 16.6 all-gather.7
  60.4 262.6 reduce-scatter.2
  327.8 142.0 all-gather.9
  500.1 719.7 all-gather.11
  1222.8 31.1 reduce-scatter.4
